TPU v7x, 256 devices: a whole 4x4x8 slice. The times are simulated.
256 devices in a mesh: dp: 32 (over x, y, core), mp: 8 (over z).
Axes of the slice: x: 4, y: 4, z: 8, core: 2. Of those that a mesh axis runs over, the one named last changes fastest.
Arguments:
- hidden: bfloat16 [49152, 5120], P('dp', 'mp'), may hold values from -6 to 6
- key_grads: bfloat16 [49152, 1024], P('dp', 'mp'), may hold values from -480 to 480
- token_ids: int32 [32, 1536], P('dp'), may hold values from 0 to 151643, as said below
- flags: int32 [32], P('dp'), may hold values from 0 to 2, as said below
- momentum: float32 [32, 5120, 1024], P('dp', 'mp'), may hold values from -8 to 8
- center: float32 [8, 640, 1024], P('mp', 'dp'), may hold values from -1.9 to 1.9
- weight: float32 [5120, 1024], P('mp'), may hold values from -0.078125 to 0.078125
Outputs:
- aggregate: float32 [8, 640, 1024], P('mp', 'dp')
- new_weight: float32 [5120, 1024], P('mp')
Inputs may be any that keep to these rules, and one draw needn't show every extreme that they name: `token_ids`: each worker's batch holds 4 sequences of 384 positions; each sequence begins with at least 96 ids below 151643 and is filled up with 151643. `flags`: exactly 8 workers have a nonzero flag.
All inputs are finite; a program needn't handle non-finite values.
Results may differ from a plain program's by a relative error of at most 0.0003.
Values may be sent and summed in bfloat16 or wider, within the bound.
A program may use at most 64 MiB of HBM per device.

v0:
```python
import math

import jax
import jax.numpy as jnp
from jax import lax
from jax.sharding import Mesh
from jax.sharding import PartitionSpec as P

D = 5120
KV = 1024
ITERS = 3
DP = ("dp_0", "dp_1", "dp_2")


pad_token = 151643
momentum_beta = 0.9
attack_gain = 8.0
clip_ratio = 0.5
learning_rate = 0.05


def sent_to_all(shard, axis):
    copies = jnp.broadcast_to(shard, (lax.axis_size(axis), *shard.shape))
    return lax.all_to_all(copies, axis, split_axis=0, concat_axis=0, tiled=True)


def over_copies(shard, axis):
    everything = sent_to_all(shard, axis)
    return jnp.sum(everything, axis=0)


def over_axes(shard, axes):
    far, near = axes
    return over_copies(over_copies(shard, near), far)


def laid_out(blocks, dim):
    shape = list(blocks.shape[1:])
    shape[dim] *= blocks.shape[0]
    return jnp.moveaxis(blocks, 0, dim).reshape(shape)


def whole_of(shard, axes, dim):
    far, near = axes
    leading = sent_to_all(shard, far)
    blocks = jnp.swapaxes(sent_to_all(leading, near), 0, 1)
    return laid_out(blocks.reshape(-1, *shard.shape), dim)


def per_device(hidden, key_grads, token_ids, flags, momentum, center, weight):
    workers = lax.axis_size(DP)
    live = token_ids[0] != pad_token
    count = jnp.sum(live.astype(jnp.float32))
    masked = jnp.where(live[:, None], key_grads, jnp.zeros_like(key_grads))
    gradient = (
        lax.dot_general(
            hidden,
            lax.all_gather(masked, "mp", axis=1, tiled=True),
            (((0,), (0,)), ((), ())),
            preferred_element_type=jnp.float32,
        )
        / count
    )
    blended = momentum_beta * momentum[0] + (1.0 - momentum_beta) * gradient
    factor = jnp.where(flags[0] == 1, attack_gain, jnp.where(flags[0] == 2, -1.0, 1.0))
    outgoing = blended * factor
    radius = clip_ratio * math.sqrt(D * KV)
    owned_rows = center.shape[1]
    blocks = outgoing.reshape(workers, owned_rows, outgoing.shape[1])
    regrouped = lax.all_to_all(blocks, DP, split_axis=0, concat_axis=0, tiled=True)
    current = center[0]
    for iteration in range(ITERS):
        offsets = regrouped - current[None]
        partial_value = jnp.sum(offsets * offsets, axis=(1, 2))
        distance = jnp.sqrt(over_axes(partial_value, (("dp_0", "dp_1"), ("dp_2", "mp"))))
        weights_now = radius / jnp.maximum(distance, radius)
        current = current + jnp.mean(weights_now[:, None, None] * offsets, axis=0)
    whole_slab = whole_of(current, (("dp_0", "dp_1"), "dp_2"), 0)
    return (current[None], weight - learning_rate * whole_slab)


def solution(mesh):
    torus = Mesh(mesh.devices.reshape(4, 4, 2, mesh.shape["mp"]), ("dp_0", "dp_1", "dp_2", "mp"))
    return jax.shard_map(
        per_device,
        mesh=torus,
        in_specs=(
            P(DP, "mp"),
            P(DP, "mp"),
            P(DP, None),
            P(DP),
            P(DP, "mp", None),
            P("mp", DP, None),
            P("mp", None),
        ),
        out_specs=(P("mp", DP, None), P("mp", None)),
        check_vma=False,
    )
```

profile of v0, /device:TPU:1, one launch (start us, length us, event | category | flops | bytes accessed | tf_op | source)
XLA Modules:
  0.0 262.4 jit_solution(15440564148938692671)
XLA Ops:
  7.2 0.0 copy-start
  7.2 0.0 all-gather.2.cloned.1.call-start
  7.2 0.9 compare_reduce_fusion
  8.1 2.0 broadcast_select_fusion
  10.1 0.0 all-gather.2.cloned.1.call-update
  10.8 0.6 convert_reduce_fusion
  11.3 53.7 %all-gather.2.cloned.1.call-done = bf16[1536,1024]{1,0:T(8,128)(2,1)} async-done(((bf16[1536,128]{1,0:T(8,128)(2,1)}), bf16[1536,1024]{1,0:T(8,128)(2,1)}) %all-gather.2.cloned.1.call-update) | async-done | bytes 3145744 | tf_op jit(solution)/shard_map/all_gather | solution.py:58
  65.1 0.0 copy-done
  65.1 7.1 %fusion = f32[640,1024]{1,0:T(8,128)} fusion(f32[1,640,1024]{2,1,0:T(8,128)} %param.11, bf16[1536,1024]{1,0:T(8,128)(2,1)} %all-gather.2.cloned.1.call-done, bf16[1536,640]{1,0:T(8,128)(2,1)S(1)} %copy-done, f32[]{:T(128)} %bitcast.2, f32[]{:T(128)} %convert_reduce_fusion), kind=kOutput, calls=%fused_computation.7 | convolution fusion | flops 2016542720 | bytes 10354696 | tf_op jit(solution)/shard_map/dot_general | solution.py:56
  72.2 4.0 %reshape.96 = f32[32,20,1024]{2,1,0:T(8,128)} reshape(f32[640,1024]{1,0:T(8,128)} %fusion) | data formatting | bytes 5242880 | tf_op jit(solution)/shard_map/reshape | solution.py:69
  76.2 0.0 copy-start.2
  76.2 12.2 %all-to-all-start = ((f32[32,20,1024]{2,1,0:T(8,128)}), f32[32,20,1024]{2,1,0:T(8,128)}, u32[]{:S(2)}, u32[]{:S(2)}) async-start(f32[32,20,1024]{2,1,0:T(8,128)} %reshape.96), calls=%async_computation | async-start | bytes 6291456 | tf_op jit(solution)/shard_map/all_to_all | solution.py:70
  88.3 0.0 copy-done.2
  88.4 39.8 %all-to-all-done = f32[32,20,1024]{2,1,0:T(8,128)} async-done(((f32[32,20,1024]{2,1,0:T(8,128)}), f32[32,20,1024]{2,1,0:T(8,128)}, u32[]{:S(2)}, u32[]{:S(2)}) %all-to-all-start) | async-done | bytes 2621472 | tf_op jit(solution)/shard_map/all_to_all | solution.py:70
  128.1 2.4 multiply_reduce_fusion.5
  130.5 12.4 %all_to_all.51 = f32[16,1,32]{2,1,0:T(1,128)S(1)} all-to-all(f32[16,1,32]{2,1,0:T(1,128)S(1)} %broadcast_in_dim.44), channel_id=1, replica_groups=mesh['dp_0'=4,'dp_1'=4,'dp_2'=2,'mp'=8] {'dp_2','mp'}, dimensions={0} | all-to-all | bytes 4096 | tf_op jit(solution)/shard_map/all_to_all | solution.py:24
  142.9 9.7 %all_to_all.52 = f32[16,1,32]{2,1,0:T(1,128)S(1)} all-to-all(f32[16,1,32]{2,1,0:T(1,128)S(1)} %broadcast_in_dim.45), channel_id=1, replica_groups=mesh['dp_0'=4,'dp_1'=4,'dp_2'=2,'mp'=8] {'dp_0','dp_1'}, dimensions={0} | all-to-all | bytes 4096 | tf_op jit(solution)/shard_map/all_to_all | solution.py:24
  152.6 2.4 multiply_reduce_fusion.4
  155.0 2.4 multiply_reduce_fusion.3
  157.4 11.5 %all_to_all.53 = f32[16,1,32]{2,1,0:T(1,128)S(1)} all-to-all(f32[16,1,32]{2,1,0:T(1,128)S(1)} %broadcast_in_dim.46), channel_id=1, replica_groups=mesh['dp_0'=4,'dp_1'=4,'dp_2'=2,'mp'=8] {'dp_2','mp'}, dimensions={0} | all-to-all | bytes 4096 | tf_op jit(solution)/shard_map/all_to_all | solution.py:24
  168.9 9.1 %all_to_all.54 = f32[16,1,32]{2,1,0:T(1,128)S(1)} all-to-all(f32[16,1,32]{2,1,0:T(1,128)S(1)} %broadcast_in_dim.47), channel_id=1, replica_groups=mesh['dp_0'=4,'dp_1'=4,'dp_2'=2,'mp'=8] {'dp_0','dp_1'}, dimensions={0} | all-to-all | bytes 4096 | tf_op jit(solution)/shard_map/all_to_all | solution.py:24
  178.1 2.4 multiply_reduce_fusion.2
  180.5 0.0 copy-start.1
  180.5 2.4 multiply_reduce_fusion.1
  182.9 11.5 %all_to_all.55 = f32[16,1,32]{2,1,0:T(1,128)S(1)} all-to-all(f32[16,1,32]{2,1,0:T(1,128)S(1)} %broadcast_in_dim.48), channel_id=1, replica_groups=mesh['dp_0'=4,'dp_1'=4,'dp_2'=2,'mp'=8] {'dp_2','mp'}, dimensions={0} | all-to-all | bytes 4096 | tf_op jit(solution)/shard_map/all_to_all | solution.py:24
  194.5 9.1 %all_to_all.56 = f32[16,1,32]{2,1,0:T(1,128)S(1)} all-to-all(f32[16,1,32]{2,1,0:T(1,128)S(1)} %broadcast_in_dim.49), channel_id=1, replica_groups=mesh['dp_0'=4,'dp_1'=4,'dp_2'=2,'mp'=8] {'dp_0','dp_1'}, dimensions={0} | all-to-all | bytes 4096 | tf_op jit(solution)/shard_map/all_to_all | solution.py:24
  203.7 2.4 multiply_reduce_fusion
  206.0 0.0 copy-done.1
  206.0 0.7 add_add_fusion
  206.7 1.3 broadcast_in_dim.50
  208.0 3.7 %all-to-all-start.7 = ((f32[16,20,1024]{2,1,0:T(8,128)}), f32[16,20,1024]{2,1,0:T(8,128)S(1)}, u32[]{:S(2)}, u32[]{:S(2)}) async-start(f32[16,20,1024]{2,1,0:T(8,128)} %broadcast_in_dim.50), calls=%async_computation.7 | async-start | bytes 3145728 | tf_op jit(solution)/shard_map/all_to_all | solution.py:24
  211.8 1.7 copy_add_fusion.1
  213.4 18.9 %all-to-all-done.7 = f32[16,20,1024]{2,1,0:T(8,128)S(1)} async-done(((f32[16,20,1024]{2,1,0:T(8,128)}), f32[16,20,1024]{2,1,0:T(8,128)S(1)}, u32[]{:S(2)}, u32[]{:S(2)}) %all-to-all-start.7) | async-done | bytes 1310752 | tf_op jit(solution)/shard_map/all_to_all | solution.py:24
  232.3 0.8 copy.32
  233.1 0.3 broadcast_in_dim.51
  233.4 9.6 %all_to_all.57 = f32[2,16,20,1024]{3,1,2,0:T(8,128)S(1)} all-to-all(f32[2,16,20,1024]{3,1,2,0:T(8,128)S(1)} %broadcast_in_dim.51), channel_id=1, replica_groups=mesh['dp_0'=4,'dp_1'=4,'dp_2'=2,'mp'=8] {'dp_2'}, dimensions={0} | all-to-all | bytes 5242880 | tf_op jit(solution)/shard_map/all_to_all | solution.py:24
  243.0 0.5 multiply_bitcast_fusion
  243.5 3.2 %copy.33 = f32[16,2,20,1024]{3,2,1,0:T(8,128)} copy(f32[16,2,20,1024]{3,0,2,1:T(8,128)S(1)} %multiply_bitcast_fusion) | data formatting | bytes 5242880 | tf_op jit(solution)/shard_map/mul | solution.py:79
  246.7 4.1 %mul.89 = f32[640,1024]{1,0:T(8,128)} reshape(f32[16,2,20,1024]{3,2,1,0:T(8,128)} %copy.33) | data formatting | bytes 5242880 | tf_op jit(solution)/shard_map/mul | solution.py:79
  250.8 4.8 %sub.42 = f32[640,1024]{1,0:T(8,128)} subtract(f32[640,1024]{1,0:T(8,128)} %param.13, f32[640,1024]{1,0:T(8,128)} %mul.89) | non-fusion elementwise | flops 655360 | bytes 7864320 | tf_op jit(solution)/shard_map/sub | solution.py:79
  (18 shorter events, 0.3 us)
Async XLA Ops:
  7.2 57.9 %copy-start = (bf16[1536,640]{1,0:T(8,128)(2,1)S(1)}, bf16[1536,640]{1,0:T(8,128)(2,1)}, u32[]{:S(2)}) copy-start(bf16[1536,640]{1,0:T(8,128)(2,1)} %param.7) | copy-start | bytes 5898244
  7.2 57.9 %all-gather.2.cloned.1.call-start = ((), (), s32[]{:S(2)}) async-start(), calls=%async_computation.9 | async-start | bytes 3538944 | tf_op jit(solution)/shard_map/all_gather | solution.py:58
  76.2 12.2 %copy-start.2 = (f32[1,20,1024]{2,0,1:T(1,128)S(1)}, f32[1,20,1024]{2,0,1:T(1,128)}, u32[]{:S(2)}) copy-start(f32[1,20,1024]{2,0,1:T(1,128)} %param.12) | copy-start | bytes 245764
  76.2 52.0 %all-to-all-start = ((f32[32,20,1024]{2,1,0:T(8,128)}), f32[32,20,1024]{2,1,0:T(8,128)}, u32[]{:S(2)}, u32[]{:S(2)}) async-start(f32[32,20,1024]{2,1,0:T(8,128)} %reshape.96), calls=%async_computation | async-start | bytes 6291456 | tf_op jit(solution)/shard_map/all_to_all | solution.py:70
  180.5 25.5 %copy-start.1 = (f32[1,20,1024]{2,1,0:T(8,128)}, f32[1,20,1024]{2,1,0:T(8,128)S(1)}, u32[]{:S(2)}) copy-start(f32[1,20,1024]{2,1,0:T(8,128)S(1)} %bitcast_add_fusion.1) | copy-start | bytes 245764
  208.0 24.3 %all-to-all-start.7 = ((f32[16,20,1024]{2,1,0:T(8,128)}), f32[16,20,1024]{2,1,0:T(8,128)S(1)}, u32[]{:S(2)}, u32[]{:S(2)}) async-start(f32[16,20,1024]{2,1,0:T(8,128)} %broadcast_in_dim.50), calls=%async_computation.7 | async-start | bytes 3145728 | tf_op jit(solution)/shard_map/all_to_all | solution.py:24
Sparse Core Ops, SparseCore 0:
  10.3 54.7 all-gather.1
where the time goes:
time: 263 us; the launch traced here: 262 us
  waiting for transfers between devices  112 us (43%)
  blocking collectives  72.9 us (28%)
  other arithmetic  25.5 us (10%)
  starting transfers between devices  15.9 us (6%)
  between operations  14.8 us (6%)
  local copies, waits for them, and re-layouts  13.8 us (5%)
  matrix products  7.14 us (3%)
    all_to_all x7, blocking collectives, sent_to_all(): return lax.all_to_all(copies, axis, split_axis=0, concat_axis=0, tiled=True)  72.9 us
    all_gather x1, waiting for transfers between devices, per_device(): lax.all_gather(masked, 'mp', axis=1, tiled=True)  53.7 us
    all_to_all x1, waiting for transfers between devices, per_device(): lax.all_to_all(blocks, DP, split_axis=0, concat_axis=0, tiled=True)  39.8 us
    all_to_all x1, waiting for transfers between devices, sent_to_all(): return lax.all_to_all(copies, axis, split_axis=0, concat_axis=0, tiled=True)  18.9 us
    all_to_all x1, starting transfers between devices, per_device(): lax.all_to_all(blocks, DP, split_axis=0, concat_axis=0, tiled=True)  12.2 us
    mul x2, local copies, waits for them, and re-layouts, per_device(): return (current[None], weight - learning_rate * whole_slab)  7.29 us
    dot_general x1, matrix products, per_device(): lax.dot_general(hidden, lax.all_gather(masked, 'mp', axis=1, tiled=True),...  7.14 us
    reduce_sum x3, other arithmetic, per_device(): partial_value = jnp.sum(offsets * offsets, axis=(1, 2))  7.12 us
  transfers between devices with their start and end apart: 3, of which 3 were waited for; matrix products, arithmetic and copies ran while one was open for 1% of the time, Pallas kernels for 0%

commit v1 on v0

v1 whole, which is shorter than its diff:
```python
import math

import jax
import jax.numpy as jnp
from jax import lax
from jax.experimental import pallas as pl
from jax.experimental.pallas import tpu as pltpu
from jax.sharding import Mesh
from jax.sharding import PartitionSpec as P

D = 5120
KV = 1024
ITERS = 3
NX, NY, NC, NZ = 4, 4, 2, 8
DP = NX * NY * NC
ROWS = D // NZ
COLS = KV // NZ
GROUPS = 8
GR = ROWS // GROUPS
OWNED = ROWS // DP
TOK = 1536
NK = 4
TK = TOK // NK

pad_token = 151643
momentum_beta = 0.9
attack_gain = 8.0
clip_ratio = 0.5
learning_rate = 0.05
radius = clip_ratio * math.sqrt(D * KV)

MESH = pl.DeviceIdType.MESH
f32 = jnp.float32
bf16 = jnp.bfloat16
HIGHEST = lax.Precision.HIGHEST


def near_first():
    def far(i):
        return min(i, NX - i)

    pairs = [(i, j) for i in range(NX) for j in range(NY) if (i, j) != (0, 0)]
    return sorted(pairs, key=lambda p: far(p[0]) + far(p[1]))


def owner_of(group, b):
    x = group >> 1
    return x, 2 * (group & 1) + ((b + x) & 1)


def kernel(
    hid, kg, tok, flag, mom, cen, wgt,
    agg, nw,
    hid_v, ht, own_k, kbuf, mom_v, acc, out_v, recv, cen_r, cen_w, wgt_v, nw_v, vs, gz, gp, gam,
    load_sem, k_recv, k_send, a_recv, a_send, c_recv, c_send, gz_recv, gz_send, gp_recv, gp_send,
    v_recv, v_send, f_recv, f_send, nw_sem,
):
    x, y, c, z = (lax.axis_index(a) for a in ("x", "y", "c", "z"))
    chip = x * NY + y
    me = chip * NC + c
    up, down = (z + 1) & 7, (z + 7) & 7

    hid_load = pltpu.make_async_copy(hid, hid_v, load_sem.at[0])
    k_load = pltpu.make_async_copy(kg, own_k, load_sem.at[1])
    mom_load = pltpu.make_async_copy(mom.at[0], mom_v, load_sem.at[2])
    wgt_load = pltpu.make_async_copy(wgt, wgt_v, load_sem.at[3])
    hid_load.start()
    k_load.start()
    mom_load.start()

    barrier = pltpu.get_barrier_semaphore()

    def plane_id(i):
        return (i >> 3, (i >> 1) & 3, i & 1, z)

    @pl.loop(0, DP)
    def _(i):
        @pl.when(i != me)
        def _():
            pl.semaphore_signal(barrier, inc=1, device_id=plane_id(i), device_id_type=MESH)

    @pl.loop(0, NZ)
    def _(i):
        @pl.when(i != z)
        def _():
            pl.semaphore_signal(barrier, inc=1, device_id=(x, y, c, i), device_id_type=MESH)

    pl.semaphore_wait(barrier, DP - 1 + NZ - 1)

    def chunk_copy(src, j, k, way, dist, target):
        return pltpu.make_async_remote_copy(
            src_ref=src,
            dst_ref=kbuf.at[j * NK + k],
            send_sem=k_send.at[way],
            recv_sem=k_recv.at[way, dist, k],
            device_id=(x, y, c, target),
            device_id_type=MESH,
        )

    def kslice(j, k):
        return kbuf.at[j * NK + k]

    for k in range(NK):
        own = kg.at[pl.ds(k * TK, TK)]
        chunk_copy(own, z, k, 0, 0, up).start()
        chunk_copy(own, z, k, 1, 0, down).start()

    c_group = x * 2 + (y >> 1)
    quarter = (y & 1) * 2 + c
    for j in range(NZ):
        b, cc, slot = (j >> 1) & 1, j >> 2, j & 1
        tx, ty = owner_of(c_group, b)
        mine = (ty == y) & (c == cc)
        src = cen.at[0, :, pl.ds(j * COLS, COLS)]

        @pl.when(mine)
        def _():
            pltpu.make_async_copy(src, cen_r.at[slot, quarter], c_recv.at[slot, quarter]).start()

        @pl.when(jnp.logical_not(mine))
        def _():
            pltpu.make_async_remote_copy(
                src_ref=src,
                dst_ref=cen_r.at[slot, quarter],
                send_sem=c_send.at[j],
                recv_sem=c_recv.at[slot, quarter],
                device_id=(tx, ty, cc, z),
                device_id_type=MESH,
            ).start()

    wgt_load.start()

    live = (tok[...] != pad_token).astype(f32)
    count = jnp.sum(live)
    kind = flag[0]
    factor = jnp.where(kind == 1, attack_gain, jnp.where(kind == 2, -1.0, 1.0)).astype(f32)
    mom_scale = factor * momentum_beta
    grad_scale = factor * (1.0 - momentum_beta) / count
    mask = live.astype(bf16)

    hid_load.wait()
    for k in range(NK):
        part = jnp.transpose(hid_v[pl.ds(k * TK, TK), :])
        ht[k] = part * mask[:, k * TK:(k + 1) * TK]

    def finish(j, value):
        columns = pl.ds(pl.multiple_of(j * COLS, COLS), COLS)
        sent = mom_scale * mom_v[:, columns] + grad_scale * value
        out_v[pl.ds(j * GROUPS, GROUPS)] = sent.reshape(GROUPS, GR, COLS)
        b, cc, slot = (j >> 1) & 1, j >> 2, j & 1

        @pl.loop(0, GROUPS)
        def _(group):
            tx, ty = owner_of(group, b)
            mine = (tx == x) & (ty == y) & (cc == c)

            @pl.when(mine)
            def _():
                pltpu.make_async_copy(
                    out_v.at[j * GROUPS + group], recv.at[slot, me], a_recv.at[slot]
                ).start()

            @pl.when(jnp.logical_not(mine))
            def _():
                pltpu.make_async_remote_copy(
                    src_ref=out_v.at[j * GROUPS + group],
                    dst_ref=recv.at[slot, me],
                    send_sem=a_send,
                    recv_sem=a_recv.at[slot],
                    device_id=(tx, ty, cc, z),
                    device_id_type=MESH,
                ).start()

    k_load.wait()
    mom_load.wait()
    acc[:, :COLS] = jnp.dot(ht[0], own_k[:TK], preferred_element_type=f32)
    for k in range(1, NK):
        acc[:, :COLS] += jnp.dot(ht[k], own_k[k * TK:(k + 1) * TK], preferred_element_type=f32)
    finish(z, acc[:, :COLS])

    @pl.loop(0, 3 * NK)
    def _(t):
        dist, k = 1 + (t >> 2), t & 3
        j_up, j_down = (z - dist + 8) & 7, (z + dist) & 7
        arrived = chunk_copy(kslice(j_up, k), j_up, k, 0, dist - 1, up)
        arrived.wait_recv()

        @pl.when((dist < 3) | (k < 2))
        def _():
            chunk_copy(kslice(j_up, k), j_up, k, 0, dist, up).start()

        arrived = chunk_copy(kslice(j_down, k), j_down, k, 1, dist - 1, down)
        arrived.wait_recv()

        @pl.when((dist < 3) | (k >= 2))
        def _():
            chunk_copy(kslice(j_down, k), j_down, k, 1, dist, down).start()

        both = jnp.concatenate([kbuf[j_up * NK + k], kbuf[j_down * NK + k]], axis=1)
        product = jnp.dot(ht[k], both, preferred_element_type=f32)

        @pl.when(k == 0)
        def _():
            acc[...] = product

        @pl.when(k > 0)
        def _():
            acc[...] += product

        @pl.when(k == NK - 1)
        def _():
            finish(j_up, acc[:, :COLS])
            finish(j_down, acc[:, COLS:])

    far = (z + 4) & 7
    for k in range(2):
        chunk_copy(kslice(far, k), far, k, 0, 3, up).wait_recv()
        chunk_copy(kslice(far, k + 2), far, k + 2, 1, 3, down).wait_recv()
        part = jnp.dot(ht[k], kbuf[far * NK + k], preferred_element_type=f32)
        part += jnp.dot(ht[k + 2], kbuf[far * NK + k + 2], preferred_element_type=f32)
        if k == 0:
            acc[:, :COLS] = part
        else:
            acc[:, :COLS] += part
    finish(far, acc[:, :COLS])

    for slot in range(2):
        for q in range(4):
            pltpu.make_async_copy(cen_r.at[slot, q], cen_r.at[slot, q], c_recv.at[slot, q]).wait()
            cen_w[slot, q * OWNED:(q + 1) * OWNED, :] = cen_r[slot, q]

    first = (z + 1) & 1
    gram = None
    for turn in range(2):
        slot = (first + turn) & 1
        pltpu.make_async_copy(recv.at[slot], recv.at[slot], a_recv.at[slot]).wait()

        def body(i, total):
            halves = []
            for h in range(2):
                r = pl.ds(pl.multiple_of(i * 16 + h * 8, 8), 8)
                offset = recv[slot, :, r, :] - cen_w[slot, r, :][None]
                halves.append(offset.reshape(DP * 8, COLS))
            both = jnp.concatenate(halves, axis=1)
            hi = both.astype(bf16)
            lo = (both - hi.astype(f32)).astype(bf16)
            nt = (((1,), (1,)), ((), ()))
            total = total + lax.dot_general(hi, hi, nt, preferred_element_type=f32)
            total = total + lax.dot_general(hi, lo, nt, preferred_element_type=f32)
            total = total + lax.dot_general(lo, hi, nt, preferred_element_type=f32)
            return total

        start = jnp.zeros((DP * 8, DP * 8), f32) if gram is None else gram
        gram = lax.fori_loop(0, GR // 16, body, start)

    ii = lax.broadcasted_iota(jnp.int32, (DP * 8, DP * 8), 0)
    jj = lax.broadcasted_iota(jnp.int32, (DP * 8, DP * 8), 1)
    gram = jnp.where((ii & 7) == (jj & 7), gram, 0.0)
    gram = jnp.sum(gram.reshape(DP, 8, DP * 8), axis=1)
    fold = (
        (lax.broadcasted_iota(jnp.int32, (DP * 8, COLS), 0) >> 3)
        == lax.broadcasted_iota(jnp.int32, (DP * 8, COLS), 1)
    ).astype(f32)
    gram = jnp.dot(gram, fold, precision=HIGHEST, preferred_element_type=f32)
    packed = gram[0:8]
    for q in range(1, 4):
        packed = packed + pltpu.roll(gram[q * 8:(q + 1) * 8], q * DP, 1)

    gz[z] = packed

    @pl.loop(1, NZ)
    def _(i):
        pltpu.make_async_remote_copy(
            src_ref=gz.at[z],
            dst_ref=gz.at[z],
            send_sem=gz_send,
            recv_sem=gz_recv,
            device_id=(x, y, c, (z + i) & 7),
            device_id_type=MESH,
        ).start()

    pltpu.make_async_copy(gz.at[pl.ds(0, NZ - 1)], gz.at[pl.ds(0, NZ - 1)], gz_recv).wait()
    gp[me] = jnp.sum(gz[...], axis=0)

    @pl.loop(1, DP)
    def _(i):
        pltpu.make_async_remote_copy(
            src_ref=gp.at[me],
            dst_ref=gp.at[me],
            send_sem=gp_send,
            recv_sem=gp_recv,
            device_id=plane_id((me + i) & (DP - 1)),
            device_id_type=MESH,
        ).start()

    pltpu.make_async_copy(gp.at[pl.ds(0, DP - 1)], gp.at[pl.ds(0, DP - 1)], gp_recv).wait()
    packed = jnp.sum(gp[...], axis=0)
    lane8 = lax.broadcasted_iota(jnp.int32, (8, COLS), 1)
    pieces = []
    for q in range(4):
        piece = packed if q == 0 else pltpu.roll(packed, COLS - q * DP, 1)
        pieces.append(jnp.where(lane8 < DP, piece, 0.0))
    gram = jnp.concatenate(pieces, axis=0)

    row = lax.broadcasted_iota(jnp.int32, (DP, COLS), 0)
    lane = lax.broadcasted_iota(jnp.int32, (DP, COLS), 1)
    diag = jnp.where(row == lane, gram, 0.0)
    diag_col = jnp.sum(diag, axis=1, keepdims=True)
    diag_row = jnp.sum(diag, axis=0, keepdims=True)
    in_row = lane[:1] < DP
    w_col = jnp.zeros((DP, 1), f32)
    w_row = jnp.zeros((1, COLS), f32)
    for iteration in range(ITERS):
        if iteration == 0:
            sq_col, sq_row = diag_col, diag_row
        else:
            g_col = jnp.sum(gram * w_row, axis=1, keepdims=True)
            g_row = jnp.sum(gram * w_col, axis=0, keepdims=True)
            quad = jnp.sum(g_row * w_row, axis=1, keepdims=True)
            sq_col = diag_col - 2.0 * g_col + quad
            sq_row = diag_row - 2.0 * g_row + quad
        coef_col = radius / jnp.maximum(jnp.sqrt(jnp.maximum(sq_col, 0.0)), radius)
        coef_row = radius / jnp.maximum(jnp.sqrt(jnp.maximum(sq_row, 0.0)), radius)
        coef_row = jnp.where(in_row, coef_row, 0.0)
        mean = jnp.sum(coef_row, axis=1, keepdims=True) * (1.0 / DP)
        w_col = (1.0 - mean) * w_col + coef_col * (1.0 / DP)
        w_row = (1.0 - mean) * w_row + coef_row * (1.0 / DP)
    gam[...] = jnp.broadcast_to(w_col, (DP, COLS))
    keep = 1.0 - jnp.sum(w_row, axis=1, keepdims=True)

    for slot in range(2):
        total = keep * cen_w[slot]
        for w in range(DP):
            total = total + gam[w:w + 1, :] * recv[slot, w]
        vs[c, chip, slot] = total

    order = near_first()
    for dx, dy in order:
        pltpu.make_async_remote_copy(
            src_ref=vs.at[c, chip],
            dst_ref=vs.at[c, chip],
            send_sem=v_send,
            recv_sem=v_recv.at[chip],
            device_id=((x + dx) & 3, (y + dy) & 3, c, z),
            device_id_type=MESH,
        ).start()

    wgt_load.wait()

    def forward(p):
        return pltpu.make_async_remote_copy(
            src_ref=vs.at[c, p],
            dst_ref=vs.at[c, p],
            send_sem=f_send,
            recv_sem=f_recv.at[p],
            device_id=(x, y, 1 - c, z),
            device_id_type=MESH,
        )

    def place(core, p):
        px, py = p >> 2, p & 3
        rows = pl.ds(pl.multiple_of((px * 2 + (py >> 1)) * GR, GR), GR)
        half = 2 * core + ((px + py) & 1)
        for slot in range(2):
            columns = pl.ds(pl.multiple_of(half * 2 * COLS + slot * COLS, COLS), COLS)
            nw_v[rows, columns] = wgt_v[rows, columns] - learning_rate * vs[core, p, slot]
        both = pl.ds(pl.multiple_of(half * 2 * COLS, 2 * COLS), 2 * COLS)
        pltpu.make_async_copy(nw_v.at[rows, both], nw.at[rows, both], nw_sem).start()

    forward(chip).start()
    place(c, chip)
    for dx, dy in order:
        p = ((x - dx) & 3) * NY + ((y - dy) & 3)
        pltpu.make_async_copy(vs.at[c, p], vs.at[c, p], v_recv.at[p]).wait()
        forward(p).start()
        place(c, p)
    for dx, dy in [(0, 0)] + order:
        p = ((x - dx) & 3) * NY + ((y - dy) & 3)
        pltpu.make_async_copy(vs.at[1 - c, p], vs.at[1 - c, p], f_recv.at[p]).wait()
        place(1 - c, p)

    for cc in range(NC):
        for b in range(2):
            px, py = owner_of(c_group, b)
            for slot in range(2):
                j = cc * 4 + b * 2 + slot
                for q in range(4):
                    @pl.when(quarter == q)
                    def _():
                        agg[0, :, j * COLS:(j + 1) * COLS] = vs[
                            cc, px * NY + py, slot, q * OWNED:(q + 1) * OWNED, :
                        ]

    pltpu.make_async_copy(nw_v, nw, nw_sem).wait()
    for way in range(2):
        part = kbuf.at[pl.ds(0, 14)]
        pltpu.make_async_copy(part, part, k_send.at[way]).wait()
    sent = out_v.at[pl.ds(0, NZ * GROUPS - 2)]
    pltpu.make_async_copy(sent, sent, a_send).wait()
    for j in range(NZ):
        tx, ty = owner_of(c_group, (j >> 1) & 1)

        @pl.when(jnp.logical_not((ty == y) & (c == (j >> 2))))
        def _():
            pltpu.make_async_copy(cen_r.at[0, 0], cen_r.at[0, 0], c_send.at[j]).wait()
    pltpu.make_async_copy(gz.at[pl.ds(0, NZ - 1)], gz.at[pl.ds(0, NZ - 1)], gz_send).wait()
    pltpu.make_async_copy(gp.at[pl.ds(0, DP - 1)], gp.at[pl.ds(0, DP - 1)], gp_send).wait()
    pltpu.make_async_copy(vs.at[0, pl.ds(0, 15)], vs.at[0, pl.ds(0, 15)], v_send).wait()
    pltpu.make_async_copy(vs.at[0], vs.at[0], f_send).wait()


def per_device(hidden, key_grads, token_ids, flags, momentum, center, weight):
    hbm = pl.BlockSpec(memory_space=pl.ANY)
    vmem = pl.BlockSpec(memory_space=pltpu.VMEM)
    dma = pltpu.SemaphoreType.DMA
    return pl.pallas_call(
        kernel,
        out_shape=(
            jax.ShapeDtypeStruct((1, OWNED, KV), f32),
            jax.ShapeDtypeStruct((ROWS, KV), f32),
        ),
        in_specs=[hbm, hbm, vmem, pl.BlockSpec(memory_space=pltpu.SMEM), hbm, hbm, hbm],
        out_specs=(vmem, hbm),
        scratch_shapes=[
            pltpu.VMEM((TOK, ROWS), bf16),
            pltpu.VMEM((NK, ROWS, TK), bf16),
            pltpu.VMEM((TOK, COLS), bf16),
            pltpu.VMEM((NZ * NK, TK, COLS), bf16),
            pltpu.VMEM((ROWS, KV), f32),
            pltpu.VMEM((ROWS, 2 * COLS), f32),
            pltpu.VMEM((NZ * GROUPS, GR, COLS), f32),
            pltpu.VMEM((2, DP, GR, COLS), f32),
            pltpu.VMEM((2, 4, OWNED, COLS), f32),
            pltpu.VMEM((2, GR, COLS), f32),
            pltpu.VMEM((ROWS, KV), f32),
            pltpu.VMEM((ROWS, KV), f32),
            pltpu.VMEM((NC, NX * NY, 2, GR, COLS), f32),
            pltpu.VMEM((NZ, 8, COLS), f32),
            pltpu.VMEM((DP, 8, COLS), f32),
            pltpu.VMEM((DP, COLS), f32),
            dma((4,)),
            dma((2, 4, NK)),
            dma((2,)),
            dma((2,)),
            dma,
            dma((2, 4)),
            dma((NZ,)),
            dma,
            dma,
            dma,
            dma,
            dma((NX * NY,)),
            dma,
            dma((NX * NY,)),
            dma,
            dma,
        ],
        compiler_params=pltpu.CompilerParams(collective_id=0, has_side_effects=True),
        name="clip",
    )(hidden, key_grads, token_ids, flags, momentum, center, weight)


def solution(mesh):
    torus = Mesh(mesh.devices.reshape(NX, NY, NC, NZ), ("x", "y", "c", "z"))
    dp = ("x", "y", "c")
    return jax.shard_map(
        per_device,
        mesh=torus,
        in_specs=(
            P(dp, "z"),
            P(dp, "z"),
            P(dp, None),
            P(dp),
            P(dp, "z", None),
            P("z", dp, None),
            P("z", None),
        ),
        out_specs=(P("z", dp, None), P("z", None)),
        check_vma=False,
    )
```

time: 263 us -> 100 us (0.38)
  waiting for transfers between devices: 112 us -> 0 us
  Pallas kernels: 0 us -> 91.9 us
  blocking collectives: 72.9 us -> 0 us
  other arithmetic: 25.5 us -> 0 us
  starting transfers between devices: 15.9 us -> 0 us
  between operations: 14.8 us -> 1.29 us
  matrix products: 7.14 us -> 0 us
  local copies, waits for them, and re-layouts: 13.8 us -> 6.72 us
    pallas_call x0 -> x1, Pallas kernels: none -> 91.9 us  [per_device(): pl.pallas_call(kernel, out_shape=(jax.ShapeDtypeStruct((1, OWNED, KV), f3...]
    all_to_all x7 -> x0, blocking collectives: 72.9 us -> none  [sent_to_all(): return lax.all_to_all(copies, axis, split_axis=0, concat_axis=0, tiled=True)]
    all_to_all x2 -> x0, waiting for transfers between devices: 58.6 us -> none  [the longest x1 39.8 us: per_device(): lax.all_to_all(blocks, DP, split_axis=0, concat_axis=0, tiled=True)]
    all_gather x1 -> x0, waiting for transfers between devices: 53.7 us -> none  [per_device(): lax.all_gather(masked, 'mp', axis=1, tiled=True)]
    all_to_all x2 -> x0, starting transfers between devices: 15.9 us -> none  [the longest x1 12.2 us: per_device(): lax.all_to_all(blocks, DP, split_axis=0, concat_axis=0, tiled=True)]
    reduce_sum x13 -> x0, other arithmetic: 14.9 us -> none  [the longest x3 7.12 us: per_device(): partial_value = jnp.sum(offsets * offsets, axis=(1, 2))]
    mul x2 -> x0, local copies, waits for them, and re-layouts: 7.29 us -> none  [per_device(): return (current[None], weight - learning_rate * whole_slab)]
    dot_general x1 -> x0, matrix products: 7.14 us -> none  [per_device(): lax.dot_general(hidden, lax.all_gather(masked, 'mp', axis=1, tiled=True),...]
  transfers between devices with their start and end apart: 3 -> 0, of which waited for: 3 -> 0; matrix products, arithmetic and copies ran while one was open for 1% -> 0% of each run, Pallas kernels for 0% -> 0%
where the time goes in v1:
time: 100 us; the launch traced here: 99.9 us
  Pallas kernels  91.9 us (92%)
  local copies, waits for them, and re-layouts  6.72 us (7%)
  between operations  1.29 us (1%)
    pallas_call x1, Pallas kernels, per_device(): pl.pallas_call(kernel, out_shape=(jax.ShapeDtypeStruct((1, OWNED, KV), f3...  91.9 us
    unnamed x2, local copies, waits for them, and re-layouts  5.1 us

profile of v1, /device:TPU:1, one launch (start us, length us, event | category | flops | bytes accessed | tf_op | source)
XLA Modules:
  0.0 99.9 jit_solution(14391707772567622796)
XLA Ops:
  1.3 1.5 %copy.9.cen = f32[1,20,1024]{2,1,0:T(8,128)} copy(f32[1,20,1024]{2,0,1:T(1,128)} %param.12) | data formatting | bytes 163840 | tf_op args[5]
  2.8 91.9 %clip.1 = (f32[1,20,1024]{2,1,0:T(8,128)}, f32[640,1024]{1,0:T(8,128)}) custom-call(bf16[1536,640]{1,0:T(8,128)(2,1)} %hid.1, bf16[1536,128]{1,0:T(8,128)(2,1)} %kg.1, s32[1,1536]{1,0:T(1,128)} %tok.1, s32[1]{0:T(128)S(6)} %copy.12.flag, f32[1,640,1024]{2,1,0:T(8,128)} %mom.1, f32[1,20,1024]{2,1,0:T(8,128)} %copy.9.cen, f32[640,1024]{1,0:T(8,128)} %wgt.1), custom_call_target="tpu_custom_call" | custom-call | tf_op jit(solution)/shard_map/clip/pallas_call | solution.py:416
  94.8 1.6 %copy.10 = f32[1,20,1024]{2,0,1:T(1,128)} copy(f32[1,20,1024]{2,1,0:T(8,128)} %get-tuple-element.2) | data formatting | bytes 163840 | tf_op jit(solution)/shard_map/clip/pallas_call | solution.py:416
  96.4 3.6 %copy.13 = f32[640,1024]{1,0:T(8,128)} copy(f32[640,1024]{1,0:T(8,128)} %get-tuple-element.7) | data formatting | bytes 5242880

commit v2 on v1

--- a/solution.py
+++ b/solution.py
@@ -32,6 +32,8 @@
 MESH = pl.DeviceIdType.MESH
 f32 = jnp.float32
 bf16 = jnp.bfloat16
+i16 = jnp.int16
+MR = GR + 8
 HIGHEST = lax.Precision.HIGHEST
 
 
@@ -43,6 +45,18 @@
     return sorted(pairs, key=lambda p: far(p[0]) + far(p[1]))
 
 
+def encode(values):
+    top = jnp.max(jnp.abs(values), axis=1, keepdims=True)
+    code = jnp.ceil(256.0 * jnp.log2(jnp.maximum(top, 2.0 ** -100)) + 0.0625)
+    steps = jnp.round(values * (32767.0 / jnp.exp2(code * (1.0 / 256.0))))
+    code = jnp.broadcast_to(code, (values.shape[0], 8, COLS))
+    return steps.astype(jnp.int32).astype(i16), code.astype(jnp.int32).astype(i16)
+
+
+def step_of(code):
+    return jnp.exp2(code.astype(jnp.int32).astype(f32) * (1.0 / 256.0)) * (1.0 / 32767.0)
+
+
 def owner_of(group, b):
     x = group >> 1
     return x, 2 * (group & 1) + ((b + x) & 1)
@@ -51,7 +65,7 @@
 def kernel(
     hid, kg, tok, flag, mom, cen, wgt,
     agg, nw,
-    hid_v, ht, own_k, kbuf, mom_v, acc, out_v, recv, cen_r, cen_w, wgt_v, nw_v, vs, gz, gp, gam,
+hid_v, ht, own_k, cen_v, cen_j, kbuf, mom_v, acc, out_v, recv, scl, cen_r, cen_w, wgt_v, nw_v, vs, gz, gp, gam,
     load_sem, k_recv, k_send, a_recv, a_send, c_recv, c_send, gz_recv, gz_send, gp_recv, gp_send,
     v_recv, v_send, f_recv, f_send, nw_sem,
 ):
@@ -63,7 +77,9 @@
     hid_load = pltpu.make_async_copy(hid, hid_v, load_sem.at[0])
     k_load = pltpu.make_async_copy(kg, own_k, load_sem.at[1])
     mom_load = pltpu.make_async_copy(mom.at[0], mom_v, load_sem.at[2])
+    cen_load = pltpu.make_async_copy(cen, cen_v, load_sem.at[4])
     wgt_load = pltpu.make_async_copy(wgt, wgt_v, load_sem.at[3])
+    cen_load.start()
     hid_load.start()
     k_load.start()
     mom_load.start()
@@ -107,11 +123,14 @@
 
     c_group = x * 2 + (y >> 1)
     quarter = (y & 1) * 2 + c
+    cen_load.wait()
+    for j in range(NZ):
+        cen_j[j] = cen_v[:, j, :]
     for j in range(NZ):
         b, cc, slot = (j >> 1) & 1, j >> 2, j & 1
         tx, ty = owner_of(c_group, b)
         mine = (ty == y) & (c == cc)
-        src = cen.at[0, :, pl.ds(j * COLS, COLS)]
+        src = cen_j.at[j]
 
         @pl.when(mine)
         def _():
@@ -146,7 +165,9 @@
     def finish(j, value):
         columns = pl.ds(pl.multiple_of(j * COLS, COLS), COLS)
         sent = mom_scale * mom_v[:, columns] + grad_scale * value
-        out_v[pl.ds(j * GROUPS, GROUPS)] = sent.reshape(GROUPS, GR, COLS)
+        steps, code = encode(sent.reshape(GROUPS, GR, COLS))
+        out_v[pl.ds(j * GROUPS, GROUPS), :GR] = steps
+        out_v[pl.ds(j * GROUPS, GROUPS), GR:] = code
         b, cc, slot = (j >> 1) & 1, j >> 2, j & 1
 
         @pl.loop(0, GROUPS)
@@ -235,11 +256,14 @@
         slot = (first + turn) & 1
         pltpu.make_async_copy(recv.at[slot], recv.at[slot], a_recv.at[slot]).wait()
 
+        scl[slot] = step_of(recv[slot, :, GR:, :])
+
         def body(i, total):
             halves = []
             for h in range(2):
                 r = pl.ds(pl.multiple_of(i * 16 + h * 8, 8), 8)
-                offset = recv[slot, :, r, :] - cen_w[slot, r, :][None]
+                steps = recv[slot, :, r, :].astype(jnp.int32).astype(f32)
+                offset = steps * scl[slot] - cen_w[slot, r, :][None]
                 halves.append(offset.reshape(DP * 8, COLS))
             both = jnp.concatenate(halves, axis=1)
             hi = both.astype(bf16)
@@ -329,10 +353,13 @@
     keep = 1.0 - jnp.sum(w_row, axis=1, keepdims=True)
 
     for slot in range(2):
-        total = keep * cen_w[slot]
+        total = (keep * cen_w[slot]).reshape(GR // 8, 8, COLS)
         for w in range(DP):
-            total = total + gam[w:w + 1, :] * recv[slot, w]
-        vs[c, chip, slot] = total
+            steps = recv[slot, w, :GR].astype(jnp.int32).astype(f32).reshape(GR // 8, 8, COLS)
+            total = total + (gam[w:w + 1, :] * scl[slot, w])[None] * steps
+        steps, code = encode(total.reshape(1, GR, COLS))
+        vs[c, chip, slot, :GR] = steps[0]
+        vs[c, chip, slot, GR:] = code[0]
 
     order = near_first()
     for dx, dy in order:
@@ -357,13 +384,17 @@
             device_id_type=MESH,
         )
 
+    def decode(core, p, slot):
+        steps = vs[core, p, slot, :GR].astype(jnp.int32).astype(f32).reshape(GR // 8, 8, COLS)
+        return (steps * step_of(vs[core, p, slot, GR:])[None]).reshape(GR, COLS)
+
     def place(core, p):
         px, py = p >> 2, p & 3
         rows = pl.ds(pl.multiple_of((px * 2 + (py >> 1)) * GR, GR), GR)
         half = 2 * core + ((px + py) & 1)
         for slot in range(2):
             columns = pl.ds(pl.multiple_of(half * 2 * COLS + slot * COLS, COLS), COLS)
-            nw_v[rows, columns] = wgt_v[rows, columns] - learning_rate * vs[core, p, slot]
+            nw_v[rows, columns] = wgt_v[rows, columns] - learning_rate * decode(core, p, slot)
         both = pl.ds(pl.multiple_of(half * 2 * COLS, 2 * COLS), 2 * COLS)
         pltpu.make_async_copy(nw_v.at[rows, both], nw.at[rows, both], nw_sem).start()
 
@@ -384,12 +415,11 @@
             px, py = owner_of(c_group, b)
             for slot in range(2):
                 j = cc * 4 + b * 2 + slot
+                rows = decode(cc, px * NY + py, slot)
                 for q in range(4):
                     @pl.when(quarter == q)
                     def _():
-                        agg[0, :, j * COLS:(j + 1) * COLS] = vs[
-                            cc, px * NY + py, slot, q * OWNED:(q + 1) * OWNED, :
-                        ]
+                        agg[:, j, :] = rows[q * OWNED:(q + 1) * OWNED]
 
     pltpu.make_async_copy(nw_v, nw, nw_sem).wait()
     for way in range(2):
@@ -410,35 +440,43 @@
 
 
 def per_device(hidden, key_grads, token_ids, flags, momentum, center, weight):
-    hbm = pl.BlockSpec(memory_space=pl.ANY)
+    hidden, key_grads, momentum, center, weight = (
+        pltpu.with_memory_space_constraint(a, pltpu.HBM)
+        for a in (hidden, key_grads, momentum, center.reshape(OWNED, NZ, COLS), weight)
+    )
+    hbm = pl.BlockSpec(memory_space=pltpu.HBM)
+    anywhere = pl.BlockSpec(memory_space=pl.ANY)
     vmem = pl.BlockSpec(memory_space=pltpu.VMEM)
     dma = pltpu.SemaphoreType.DMA
-    return pl.pallas_call(
+    aggregate, new_weight = pl.pallas_call(
         kernel,
         out_shape=(
-            jax.ShapeDtypeStruct((1, OWNED, KV), f32),
+            jax.ShapeDtypeStruct((OWNED, NZ, COLS), f32),
             jax.ShapeDtypeStruct((ROWS, KV), f32),
         ),
         in_specs=[hbm, hbm, vmem, pl.BlockSpec(memory_space=pltpu.SMEM), hbm, hbm, hbm],
-        out_specs=(vmem, hbm),
+        out_specs=(vmem, anywhere),
         scratch_shapes=[
             pltpu.VMEM((TOK, ROWS), bf16),
             pltpu.VMEM((NK, ROWS, TK), bf16),
             pltpu.VMEM((TOK, COLS), bf16),
+            pltpu.VMEM((OWNED, NZ, COLS), f32),
+            pltpu.VMEM((NZ, OWNED, COLS), f32),
             pltpu.VMEM((NZ * NK, TK, COLS), bf16),
             pltpu.VMEM((ROWS, KV), f32),
             pltpu.VMEM((ROWS, 2 * COLS), f32),
-            pltpu.VMEM((NZ * GROUPS, GR, COLS), f32),
-            pltpu.VMEM((2, DP, GR, COLS), f32),
+            pltpu.VMEM((NZ * GROUPS, MR, COLS), i16),
+            pltpu.VMEM((2, DP, MR, COLS), i16),
+            pltpu.VMEM((2, DP, 8, COLS), f32),
             pltpu.VMEM((2, 4, OWNED, COLS), f32),
             pltpu.VMEM((2, GR, COLS), f32),
             pltpu.VMEM((ROWS, KV), f32),
             pltpu.VMEM((ROWS, KV), f32),
-            pltpu.VMEM((NC, NX * NY, 2, GR, COLS), f32),
+            pltpu.VMEM((NC, NX * NY, 2, MR, COLS), i16),
             pltpu.VMEM((NZ, 8, COLS), f32),
             pltpu.VMEM((DP, 8, COLS), f32),
             pltpu.VMEM((DP, COLS), f32),
-            dma((4,)),
+            dma((5,)),
             dma((2, 4, NK)),
             dma((2,)),
             dma((2,)),
@@ -455,9 +493,10 @@
             dma,
             dma,
         ],
-        compiler_params=pltpu.CompilerParams(collective_id=0, has_side_effects=True),
+        compiler_params=pltpu.CompilerParams(collective_id=0, has_side_effects=True, vmem_limit_bytes=40 * 1024 * 1024),
         name="clip",
     )(hidden, key_grads, token_ids, flags, momentum, center, weight)
+    return aggregate.reshape(1, OWNED, KV), new_weight
 
 
 def solution(mesh):

time: 100 us -> 81.4 us (0.81)
  Pallas kernels: 91.9 us -> 77.2 us
  local copies, waits for them, and re-layouts: 6.72 us -> 2.81 us
    pallas_call x1, Pallas kernels: 91.9 us -> 77.2 us  [per_device(): pl.pallas_call(kernel, out_shape=(jax.ShapeDtypeStruct((OWNED, NZ, COLS),...]
    unnamed x2 -> x4, local copies, waits for them, and re-layouts: 5.1 us -> 2.81 us
    pallas_call x1 -> x0, local copies, waits for them, and re-layouts: 1.61 us -> none  [per_device(): pl.pallas_call(kernel, out_shape=(jax.ShapeDtypeStruct((1, OWNED, KV), f3...]
where the time goes in v2:
time: 81.4 us; the launch traced here: 81.3 us
  Pallas kernels  77.2 us (95%)
  local copies, waits for them, and re-layouts  2.81 us (3%)
  between operations  1.29 us (2%)
    pallas_call x1, Pallas kernels, per_device(): pl.pallas_call(kernel, out_shape=(jax.ShapeDtypeStruct((OWNED, NZ, COLS),...  77.2 us
    unnamed x4, local copies, waits for them, and re-layouts  2.81 us

profile of v2, /device:TPU:1, one launch (start us, length us, event | category | flops | bytes accessed | tf_op | source)
XLA Modules:
  0.0 81.3 jit_solution(927275719659684428)
XLA Ops:
  1.3 0.0 copy-start
  1.3 0.7 copy-done
  2.0 77.2 %clip.1 = (f32[20,8,128]{2,1,0:T(8,128)S(1)}, f32[640,1024]{1,0:T(8,128)S(1)}) custom-call(bf16[1536,640]{1,0:T(8,128)(2,1)} %hid.1, bf16[1536,128]{1,0:T(8,128)(2,1)} %kg.1, s32[1,1536]{1,0:T(1,128)S(1)} %copy-done, s32[1]{0:T(128)S(6)} %copy.13.flag, f32[1,640,1024]{2,1,0:T(8,128)} %mom.1, f32[20,8,128]{2,1,0:T(8,128)} %bitcast.3, f32[640,1024]{1,0:T(8,128)} %wgt.1), custom_call_target="tpu_custom_call" | custom-call | tf_op jit(solution)/shard_map/clip/pallas_call | solution.py:451
  79.2 0.6 copy.14
  79.8 1.5 %copy.15 = f32[640,1024]{1,0:T(8,128)} copy(f32[640,1024]{1,0:T(8,128)S(1)} %get-tuple-element.13) | data formatting | bytes 5242880
Async XLA Ops:
  1.3 0.7 copy-start

commit v3 on v2

--- a/solution.py
+++ b/solution.py
@@ -37,14 +37,6 @@
 HIGHEST = lax.Precision.HIGHEST
 
 
-def near_first():
-    def far(i):
-        return min(i, NX - i)
-
-    pairs = [(i, j) for i in range(NX) for j in range(NY) if (i, j) != (0, 0)]
-    return sorted(pairs, key=lambda p: far(p[0]) + far(p[1]))
-
-
 def encode(values):
     top = jnp.max(jnp.abs(values), axis=1, keepdims=True)
     code = jnp.ceil(256.0 * jnp.log2(jnp.maximum(top, 2.0 ** -100)) + 0.0625)
@@ -65,9 +57,9 @@
 def kernel(
     hid, kg, tok, flag, mom, cen, wgt,
     agg, nw,
-hid_v, ht, own_k, cen_v, cen_j, kbuf, mom_v, acc, out_v, recv, scl, cen_r, cen_w, wgt_v, nw_v, vs, gz, gp, gam,
-    load_sem, k_recv, k_send, a_recv, a_send, c_recv, c_send, gz_recv, gz_send, gp_recv, gp_send,
-    v_recv, v_send, f_recv, f_send, nw_sem,
+    tok_v, hid_v, ht, own_k, cen_v, cen_j, kbuf, mom_v, acc, out_v, recv, scl, cen_r, cen_w, wgt_v, nw_v, vs, gx, gy, gz, agg_v, gam,
+    load_sem, k_recv, k_send, a_recv, a_send, c_recv, c_send, g_recv, g_send,
+    v_recv, v_send, f_recv, f_send, nw_sem, here,
 ):
     x, y, c, z = (lax.axis_index(a) for a in ("x", "y", "c", "z"))
     chip = x * NY + y
@@ -78,30 +70,30 @@
     k_load = pltpu.make_async_copy(kg, own_k, load_sem.at[1])
     mom_load = pltpu.make_async_copy(mom.at[0], mom_v, load_sem.at[2])
     cen_load = pltpu.make_async_copy(cen, cen_v, load_sem.at[4])
+    tok_load = pltpu.make_async_copy(tok, tok_v, load_sem.at[5])
     wgt_load = pltpu.make_async_copy(wgt, wgt_v, load_sem.at[3])
     cen_load.start()
+    tok_load.start()
     hid_load.start()
     k_load.start()
     mom_load.start()
 
     barrier = pltpu.get_barrier_semaphore()
 
-    def plane_id(i):
-        return (i >> 3, (i >> 1) & 3, i & 1, z)
-
-    @pl.loop(0, DP)
-    def _(i):
-        @pl.when(i != me)
-        def _():
-            pl.semaphore_signal(barrier, inc=1, device_id=plane_id(i), device_id_type=MESH)
-
-    @pl.loop(0, NZ)
-    def _(i):
-        @pl.when(i != z)
-        def _():
-            pl.semaphore_signal(barrier, inc=1, device_id=(x, y, c, i), device_id_type=MESH)
-
-    pl.semaphore_wait(barrier, DP - 1 + NZ - 1)
+    beside_x = [((x + d) & 3, y, c, z) for d in (1, 3)]
+    beside_y = [(x, (y + d) & 3, c, z) for d in (1, 3)]
+    beside_z = [(x, y, c, up), (x, y, c, down)]
+    partner = (x, y, 1 - c, z)
+    for other in beside_z + beside_x + beside_y + [partner]:
+        pl.semaphore_signal(barrier, inc=1, device_id=other, device_id_type=MESH)
+    pl.semaphore_wait(barrier, 7)
+
+    def tell(i, others):
+        for other in others:
+            pl.semaphore_signal(here.at[i], inc=1, device_id=other, device_id_type=MESH)
+
+    def hear(i, others):
+        pl.semaphore_wait(here.at[i], len(others))
 
     def chunk_copy(src, j, k, way, dist, target):
         return pltpu.make_async_remote_copy(
@@ -121,35 +113,19 @@
         chunk_copy(own, z, k, 0, 0, up).start()
         chunk_copy(own, z, k, 1, 0, down).start()
 
+    tell(0, beside_x)
+
     c_group = x * 2 + (y >> 1)
     quarter = (y & 1) * 2 + c
     cen_load.wait()
     for j in range(NZ):
         cen_j[j] = cen_v[:, j, :]
-    for j in range(NZ):
-        b, cc, slot = (j >> 1) & 1, j >> 2, j & 1
-        tx, ty = owner_of(c_group, b)
-        mine = (ty == y) & (c == cc)
-        src = cen_j.at[j]
-
-        @pl.when(mine)
-        def _():
-            pltpu.make_async_copy(src, cen_r.at[slot, quarter], c_recv.at[slot, quarter]).start()
-
-        @pl.when(jnp.logical_not(mine))
-        def _():
-            pltpu.make_async_remote_copy(
-                src_ref=src,
-                dst_ref=cen_r.at[slot, quarter],
-                send_sem=c_send.at[j],
-                recv_sem=c_recv.at[slot, quarter],
-                device_id=(tx, ty, cc, z),
-                device_id_type=MESH,
-            ).start()
-
+    hear(0, beside_x)
+    tell(1, beside_y)
     wgt_load.start()
-
-    live = (tok[...] != pad_token).astype(f32)
+    tok_load.wait()
+
+    live = (tok_v[...] != pad_token).astype(f32)
     count = jnp.sum(live)
     kind = flag[0]
     factor = jnp.where(kind == 1, attack_gain, jnp.where(kind == 2, -1.0, 1.0)).astype(f32)
@@ -158,9 +134,14 @@
     mask = live.astype(bf16)
 
     hid_load.wait()
+    hear(1, beside_y)
+    tell(2, beside_y)
     for k in range(NK):
         part = jnp.transpose(hid_v[pl.ds(k * TK, TK), :])
         ht[k] = part * mask[:, k * TK:(k + 1) * TK]
+
+    hear(2, beside_y)
+    tell(3, [partner])
 
     def finish(j, value):
         columns = pl.ds(pl.multiple_of(j * COLS, COLS), COLS)
@@ -197,6 +178,29 @@
     acc[:, :COLS] = jnp.dot(ht[0], own_k[:TK], preferred_element_type=f32)
     for k in range(1, NK):
         acc[:, :COLS] += jnp.dot(ht[k], own_k[k * TK:(k + 1) * TK], preferred_element_type=f32)
+    hear(3, [partner])
+
+    for j in range(NZ):
+        b, cc, slot = (j >> 1) & 1, j >> 2, j & 1
+        tx, ty = owner_of(c_group, b)
+        mine = (ty == y) & (c == cc)
+        src = cen_j.at[j]
+
+        @pl.when(mine)
+        def _():
+            pltpu.make_async_copy(src, cen_r.at[slot, quarter], c_recv.at[slot, quarter]).start()
+
+        @pl.when(jnp.logical_not(mine))
+        def _():
+            pltpu.make_async_remote_copy(
+                src_ref=src,
+                dst_ref=cen_r.at[slot, quarter],
+                send_sem=c_send.at[j],
+                recv_sem=c_recv.at[slot, quarter],
+                device_id=(tx, ty, cc, z),
+                device_id_type=MESH,
+            ).start()
+
     finish(z, acc[:, :COLS])
 
     @pl.loop(0, 3 * NK)
@@ -290,35 +294,27 @@
     for q in range(1, 4):
         packed = packed + pltpu.roll(gram[q * 8:(q + 1) * 8], q * DP, 1)
 
-    gz[z] = packed
-
-    @pl.loop(1, NZ)
-    def _(i):
-        pltpu.make_async_remote_copy(
-            src_ref=gz.at[z],
-            dst_ref=gz.at[z],
-            send_sem=gz_send,
-            recv_sem=gz_recv,
-            device_id=(x, y, c, (z + i) & 7),
-            device_id_type=MESH,
-        ).start()
-
-    pltpu.make_async_copy(gz.at[pl.ds(0, NZ - 1)], gz.at[pl.ds(0, NZ - 1)], gz_recv).wait()
-    gp[me] = jnp.sum(gz[...], axis=0)
-
-    @pl.loop(1, DP)
-    def _(i):
-        pltpu.make_async_remote_copy(
-            src_ref=gp.at[me],
-            dst_ref=gp.at[me],
-            send_sem=gp_send,
-            recv_sem=gp_recv,
-            device_id=plane_id((me + i) & (DP - 1)),
-            device_id_type=MESH,
-        ).start()
-
-    pltpu.make_async_copy(gp.at[pl.ds(0, DP - 1)], gp.at[pl.ds(0, DP - 1)], gp_recv).wait()
-    packed = jnp.sum(gp[...], axis=0)
+    def reduce(stage, buffer, own, count, place_of):
+        buffer[own] = packed
+
+        @pl.loop(1, count)
+        def _(i):
+            pltpu.make_async_remote_copy(
+                src_ref=buffer.at[own],
+                dst_ref=buffer.at[own],
+                send_sem=g_send.at[stage],
+                recv_sem=g_recv.at[stage],
+                device_id=place_of((own + i) & (count - 1)),
+                device_id_type=MESH,
+            ).start()
+
+        others = buffer.at[pl.ds(0, count - 1)]
+        pltpu.make_async_copy(others, others, g_recv.at[stage]).wait()
+        return jnp.sum(buffer[...], axis=0)
+
+    packed = reduce(0, gx, x * 2 + c, NX * NC, lambda i: (i >> 1, y, i & 1, z))
+    packed = reduce(1, gy, y, NY, lambda i: (x, i, c, z))
+    packed = reduce(2, gz, z, NZ, lambda i: (x, y, c, i))
     lane8 = lax.broadcasted_iota(jnp.int32, (8, COLS), 1)
     pieces = []
     for q in range(4):
@@ -361,17 +357,34 @@
         vs[c, chip, slot, :GR] = steps[0]
         vs[c, chip, slot, GR:] = code[0]
 
-    order = near_first()
-    for dx, dy in order:
+    ring = (1, 3, 2)
+
+    def chip_at(first, second, sign):
+        cx = (x + sign * (first * (1 - c) + second * c)) & 3
+        cy = (y + sign * (first * c + second * (1 - c))) & 3
+        return cx, cy
+
+    def send(p, first, second):
         pltpu.make_async_remote_copy(
-            src_ref=vs.at[c, chip],
-            dst_ref=vs.at[c, chip],
+            src_ref=vs.at[c, p],
+            dst_ref=vs.at[c, p],
             send_sem=v_send,
-            recv_sem=v_recv.at[chip],
-            device_id=((x + dx) & 3, (y + dy) & 3, c, z),
+            recv_sem=v_recv.at[p],
+            device_id=(*chip_at(first, second, 1), c, z),
             device_id_type=MESH,
         ).start()
 
+    def source(first, second):
+        px, py = chip_at(first, second, -1)
+        return px * NY + py
+
+    def arrive(p):
+        pltpu.make_async_copy(vs.at[c, p], vs.at[c, p], v_recv.at[p]).wait()
+
+    for s in ring:
+        send(chip, s, 0)
+    for s in ring:
+        send(chip, 0, s)
     wgt_load.wait()
 
     def forward(p):
@@ -399,16 +412,25 @@
         pltpu.make_async_copy(nw_v.at[rows, both], nw.at[rows, both], nw_sem).start()
 
     forward(chip).start()
-    place(c, chip)
-    for dx, dy in order:
-        p = ((x - dx) & 3) * NY + ((y - dy) & 3)
-        pltpu.make_async_copy(vs.at[c, p], vs.at[c, p], v_recv.at[p]).wait()
+    for s in ring:
+        p = source(s, 0)
+        arrive(p)
+        for t in ring:
+            send(p, 0, t)
         forward(p).start()
-        place(c, p)
-    for dx, dy in [(0, 0)] + order:
-        p = ((x - dx) & 3) * NY + ((y - dy) & 3)
-        pltpu.make_async_copy(vs.at[1 - c, p], vs.at[1 - c, p], f_recv.at[p]).wait()
-        place(1 - c, p)
+    for s in (0,) + ring:
+        place(c, source(s, 0))
+    for s in (0,) + ring:
+        for t in ring:
+            p = source(s, t)
+            arrive(p)
+            forward(p).start()
+            place(c, p)
+    for s in (0,) + ring:
+        for t in (0,) + ring:
+            p = source(t, s)
+            pltpu.make_async_copy(vs.at[1 - c, p], vs.at[1 - c, p], f_recv.at[p]).wait()
+            place(1 - c, p)
 
     for cc in range(NC):
         for b in range(2):
@@ -419,8 +441,12 @@
                 for q in range(4):
                     @pl.when(quarter == q)
                     def _():
-                        agg[:, j, :] = rows[q * OWNED:(q + 1) * OWNED]
-
+                        agg_v[:, j, :] = rows[q * OWNED:(q + 1) * OWNED]
+
+    agg_out = pltpu.make_async_copy(agg_v, agg, load_sem.at[4])
+    agg_out.start()
+
+    agg_out.wait()
     pltpu.make_async_copy(nw_v, nw, nw_sem).wait()
     for way in range(2):
         part = kbuf.at[pl.ds(0, 14)]
@@ -433,20 +459,20 @@
         @pl.when(jnp.logical_not((ty == y) & (c == (j >> 2))))
         def _():
             pltpu.make_async_copy(cen_r.at[0, 0], cen_r.at[0, 0], c_send.at[j]).wait()
-    pltpu.make_async_copy(gz.at[pl.ds(0, NZ - 1)], gz.at[pl.ds(0, NZ - 1)], gz_send).wait()
-    pltpu.make_async_copy(gp.at[pl.ds(0, DP - 1)], gp.at[pl.ds(0, DP - 1)], gp_send).wait()
-    pltpu.make_async_copy(vs.at[0, pl.ds(0, 15)], vs.at[0, pl.ds(0, 15)], v_send).wait()
-    pltpu.make_async_copy(vs.at[0], vs.at[0], f_send).wait()
+    for stage, buffer, count in ((0, gx, NX * NC), (1, gy, NY), (2, gz, NZ)):
+        others = buffer.at[pl.ds(0, count - 1)]
+        pltpu.make_async_copy(others, others, g_send.at[stage]).wait()
+    pltpu.make_async_copy(vs.at[c, pl.ds(0, 15)], vs.at[c, pl.ds(0, 15)], v_send).wait()
+    pltpu.make_async_copy(vs.at[c], vs.at[c], f_send).wait()
 
 
 def per_device(hidden, key_grads, token_ids, flags, momentum, center, weight):
-    hidden, key_grads, momentum, center, weight = (
+    hidden, key_grads, token_ids, momentum, center, weight = (
         pltpu.with_memory_space_constraint(a, pltpu.HBM)
-        for a in (hidden, key_grads, momentum, center.reshape(OWNED, NZ, COLS), weight)
+        for a in (hidden, key_grads, token_ids, momentum, center.reshape(OWNED, NZ, COLS), weight)
     )
     hbm = pl.BlockSpec(memory_space=pltpu.HBM)
     anywhere = pl.BlockSpec(memory_space=pl.ANY)
-    vmem = pl.BlockSpec(memory_space=pltpu.VMEM)
     dma = pltpu.SemaphoreType.DMA
     aggregate, new_weight = pl.pallas_call(
         kernel,
@@ -454,9 +480,10 @@
             jax.ShapeDtypeStruct((OWNED, NZ, COLS), f32),
             jax.ShapeDtypeStruct((ROWS, KV), f32),
         ),
-        in_specs=[hbm, hbm, vmem, pl.BlockSpec(memory_space=pltpu.SMEM), hbm, hbm, hbm],
-        out_specs=(vmem, anywhere),
+        in_specs=[hbm, hbm, hbm, pl.BlockSpec(memory_space=pltpu.SMEM), hbm, hbm, hbm],
+        out_specs=(anywhere, anywhere),
         scratch_shapes=[
+            pltpu.VMEM((1, TOK), jnp.int32),
             pltpu.VMEM((TOK, ROWS), bf16),
             pltpu.VMEM((NK, ROWS, TK), bf16),
             pltpu.VMEM((TOK, COLS), bf16),
@@ -473,25 +500,26 @@
             pltpu.VMEM((ROWS, KV), f32),
             pltpu.VMEM((ROWS, KV), f32),
             pltpu.VMEM((NC, NX * NY, 2, MR, COLS), i16),
+            pltpu.VMEM((NX * NC, 8, COLS), f32),
+            pltpu.VMEM((NY, 8, COLS), f32),
             pltpu.VMEM((NZ, 8, COLS), f32),
-            pltpu.VMEM((DP, 8, COLS), f32),
+            pltpu.VMEM((OWNED, NZ, COLS), f32),
             pltpu.VMEM((DP, COLS), f32),
-            dma((5,)),
+            dma((6,)),
             dma((2, 4, NK)),
             dma((2,)),
             dma((2,)),
             dma,
             dma((2, 4)),
             dma((NZ,)),
-            dma,
-            dma,
-            dma,
-            dma,
+            dma((3,)),
+            dma((3,)),
             dma((NX * NY,)),
             dma,
             dma((NX * NY,)),
             dma,
             dma,
+            pltpu.SemaphoreType.REGULAR((4,)),
         ],
         compiler_params=pltpu.CompilerParams(collective_id=0, has_side_effects=True, vmem_limit_bytes=40 * 1024 * 1024),
         name="clip",

time: 81.4 us -> 78.5 us (0.964)
  Pallas kernels: 77.2 us -> 75 us
    pallas_call x1, Pallas kernels: 77.2 us -> 75 us  [per_device(): pl.pallas_call(kernel, out_shape=(jax.ShapeDtypeStruct((OWNED, NZ, COLS),...]
    unnamed x4 -> x2, local copies, waits for them, and re-layouts: 2.81 us -> 2.13 us
where the time goes in v3:
time: 78.5 us; the launch traced here: 78.4 us
  Pallas kernels  75 us (96%)
  local copies, waits for them, and re-layouts  2.13 us (3%)
  between operations  1.29 us (2%)
    pallas_call x1, Pallas kernels, per_device(): pl.pallas_call(kernel, out_shape=(jax.ShapeDtypeStruct((OWNED, NZ, COLS),...  75 us
    unnamed x2, local copies, waits for them, and re-layouts  2.13 us

profile of v3, /device:TPU:1, one launch (start us, length us, event | category | flops | bytes accessed | tf_op | source)
XLA Modules:
  0.0 78.4 jit_solution(7827924422232588221)
XLA Ops:
  1.3 75.0 %clip.1 = (f32[20,8,128]{2,1,0:T(8,128)S(1)}, f32[640,1024]{1,0:T(8,128)S(1)}) custom-call(bf16[1536,640]{1,0:T(8,128)(2,1)} %hid.1, bf16[1536,128]{1,0:T(8,128)(2,1)} %kg.1, s32[1,1536]{1,0:T(1,128)} %tok.1, s32[1]{0:T(128)S(6)} %copy.13.flag, f32[1,640,1024]{2,1,0:T(8,128)} %mom.1, f32[20,8,128]{2,1,0:T(8,128)} %bitcast.3, f32[640,1024]{1,0:T(8,128)} %wgt.1), custom_call_target="tpu_custom_call" | custom-call | tf_op jit(solution)/shard_map/clip/pallas_call | solution.py:477
  76.3 0.6 copy.14
  76.9 1.5 %copy.15 = f32[640,1024]{1,0:T(8,128)} copy(f32[640,1024]{1,0:T(8,128)S(1)} %get-tuple-element.13) | data formatting | bytes 5242880

commit v4 on v3

--- a/solution.py
+++ b/solution.py
@@ -348,6 +348,40 @@
     gam[...] = jnp.broadcast_to(w_col, (DP, COLS))
     keep = 1.0 - jnp.sum(w_row, axis=1, keepdims=True)
 
+    ring = (1, 3, 2)
+
+    def chip_at(first, second, sign):
+        cx = (x + sign * (first * (1 - c) + second * c)) & 3
+        cy = (y + sign * (first * c + second * (1 - c))) & 3
+        return cx, cy
+
+    def send(p, slot, first, second):
+        pltpu.make_async_remote_copy(
+            src_ref=vs.at[c, p, slot],
+            dst_ref=vs.at[c, p, slot],
+            send_sem=v_send,
+            recv_sem=v_recv.at[p, slot],
+            device_id=(*chip_at(first, second, 1), c, z),
+            device_id_type=MESH,
+        ).start()
+
+    def source(first, second):
+        px, py = chip_at(first, second, -1)
+        return px * NY + py
+
+    def arrive(p, slot):
+        pltpu.make_async_copy(vs.at[c, p, slot], vs.at[c, p, slot], v_recv.at[p, slot]).wait()
+
+    def forward(p, slot):
+        pltpu.make_async_remote_copy(
+            src_ref=vs.at[c, p, slot],
+            dst_ref=vs.at[c, p, slot],
+            send_sem=f_send,
+            recv_sem=f_recv.at[p, slot],
+            device_id=(x, y, 1 - c, z),
+            device_id_type=MESH,
+        ).start()
+
     for slot in range(2):
         total = (keep * cen_w[slot]).reshape(GR // 8, 8, COLS)
         for w in range(DP):
@@ -356,46 +390,13 @@
         steps, code = encode(total.reshape(1, GR, COLS))
         vs[c, chip, slot, :GR] = steps[0]
         vs[c, chip, slot, GR:] = code[0]
-
-    ring = (1, 3, 2)
-
-    def chip_at(first, second, sign):
-        cx = (x + sign * (first * (1 - c) + second * c)) & 3
-        cy = (y + sign * (first * c + second * (1 - c))) & 3
-        return cx, cy
-
-    def send(p, first, second):
-        pltpu.make_async_remote_copy(
-            src_ref=vs.at[c, p],
-            dst_ref=vs.at[c, p],
-            send_sem=v_send,
-            recv_sem=v_recv.at[p],
-            device_id=(*chip_at(first, second, 1), c, z),
-            device_id_type=MESH,
-        ).start()
-
-    def source(first, second):
-        px, py = chip_at(first, second, -1)
-        return px * NY + py
-
-    def arrive(p):
-        pltpu.make_async_copy(vs.at[c, p], vs.at[c, p], v_recv.at[p]).wait()
-
-    for s in ring:
-        send(chip, s, 0)
-    for s in ring:
-        send(chip, 0, s)
+        for s in ring:
+            send(chip, slot, s, 0)
+        for s in ring:
+            send(chip, slot, 0, s)
+        forward(chip, slot)
+
     wgt_load.wait()
-
-    def forward(p):
-        return pltpu.make_async_remote_copy(
-            src_ref=vs.at[c, p],
-            dst_ref=vs.at[c, p],
-            send_sem=f_send,
-            recv_sem=f_recv.at[p],
-            device_id=(x, y, 1 - c, z),
-            device_id_type=MESH,
-        )
 
     def decode(core, p, slot):
         steps = vs[core, p, slot, :GR].astype(jnp.int32).astype(f32).reshape(GR // 8, 8, COLS)
@@ -411,25 +412,28 @@
         both = pl.ds(pl.multiple_of(half * 2 * COLS, 2 * COLS), 2 * COLS)
         pltpu.make_async_copy(nw_v.at[rows, both], nw.at[rows, both], nw_sem).start()
 
-    forward(chip).start()
-    for s in ring:
-        p = source(s, 0)
-        arrive(p)
-        for t in ring:
-            send(p, 0, t)
-        forward(p).start()
+    for slot in range(2):
+        for s in ring:
+            p = source(s, 0)
+            arrive(p, slot)
+            for t in ring:
+                send(p, slot, 0, t)
+            forward(p, slot)
     for s in (0,) + ring:
         place(c, source(s, 0))
     for s in (0,) + ring:
         for t in ring:
             p = source(s, t)
-            arrive(p)
-            forward(p).start()
+            for slot in range(2):
+                arrive(p, slot)
+                forward(p, slot)
             place(c, p)
     for s in (0,) + ring:
         for t in (0,) + ring:
             p = source(t, s)
-            pltpu.make_async_copy(vs.at[1 - c, p], vs.at[1 - c, p], f_recv.at[p]).wait()
+            for slot in range(2):
+                other = vs.at[1 - c, p, slot]
+                pltpu.make_async_copy(other, other, f_recv.at[p, slot]).wait()
             place(1 - c, p)
 
     for cc in range(NC):
@@ -464,6 +468,17 @@
         pltpu.make_async_copy(others, others, g_send.at[stage]).wait()
     pltpu.make_async_copy(vs.at[c, pl.ds(0, 15)], vs.at[c, pl.ds(0, 15)], v_send).wait()
     pltpu.make_async_copy(vs.at[c], vs.at[c], f_send).wait()
+
+
+def write_out(agg, nw, agg_out, nw_out, sem):
+    copies = (
+        pltpu.make_async_copy(nw, nw_out, sem.at[0]),
+        pltpu.make_async_copy(agg, agg_out, sem.at[1]),
+    )
+    for copy in copies:
+        copy.start()
+    for copy in copies:
+        copy.wait()
 
 
 def per_device(hidden, key_grads, token_ids, flags, momentum, center, weight):
@@ -514,9 +529,9 @@
             dma((NZ,)),
             dma((3,)),
             dma((3,)),
-            dma((NX * NY,)),
+            dma((NX * NY, 2)),
             dma,
-            dma((NX * NY,)),
+            dma((NX * NY, 2)),
             dma,
             dma,
             pltpu.SemaphoreType.REGULAR((4,)),
@@ -524,6 +539,18 @@
         compiler_params=pltpu.CompilerParams(collective_id=0, has_side_effects=True, vmem_limit_bytes=40 * 1024 * 1024),
         name="clip",
     )(hidden, key_grads, token_ids, flags, momentum, center, weight)
+    aggregate, new_weight = pl.pallas_call(
+        write_out,
+        out_shape=(
+            jax.ShapeDtypeStruct((OWNED, NZ, COLS), f32),
+            jax.ShapeDtypeStruct((ROWS, KV), f32),
+        ),
+        in_specs=[anywhere] * 2,
+        out_specs=(hbm, hbm),
+        scratch_shapes=[dma((2,))],
+        compiler_params=pltpu.CompilerParams(vmem_limit_bytes=1024 * 1024),
+        name="write_out",
+    )(aggregate, new_weight)
     return aggregate.reshape(1, OWNED, KV), new_weight
 
 

time: 78.5 us -> 77.3 us (0.985)
  local copies, waits for them, and re-layouts: 2.13 us -> 0 us
  Pallas kernels: 75 us -> 76 us
    unnamed x2 -> x0, local copies, waits for them, and re-layouts: 2.13 us -> none
    pallas_call x0 -> x1, Pallas kernels: none -> 1.52 us  [per_device(): pl.pallas_call(write_out, out_shape=(jax.ShapeDtypeStruct((OWNED, NZ, COL...]
where the time goes in v4:
time: 77.3 us; the launch traced here: 77.2 us
  Pallas kernels  76 us (98%)
  between operations  1.28 us (2%)
    pallas_call x1, Pallas kernels, per_device(): pl.pallas_call(kernel, out_shape=(jax.ShapeDtypeStruct((OWNED, NZ, COLS),...  74.4 us

profile of v4, /device:TPU:1, one launch (start us, length us, event | category | flops | bytes accessed | tf_op | source)
XLA Modules:
  0.0 77.2 jit_solution(2306736618210490114)
XLA Ops:
  1.3 74.4 %clip.1 = (f32[20,8,128]{2,1,0:T(8,128)S(1)}, f32[640,1024]{1,0:T(8,128)S(1)}) custom-call(bf16[1536,640]{1,0:T(8,128)(2,1)} %hid.1, bf16[1536,128]{1,0:T(8,128)(2,1)} %kg.1, s32[1,1536]{1,0:T(1,128)} %tok.1, s32[1]{0:T(128)S(6)} %copy.11.flag, f32[1,640,1024]{2,1,0:T(8,128)} %mom.1, f32[20,8,128]{2,1,0:T(8,128)} %bitcast.2, f32[640,1024]{1,0:T(8,128)} %wgt.1), custom_call_target="tpu_custom_call" | custom-call | tf_op jit(solution)/shard_map/clip/pallas_call | solution.py:492
  75.7 1.5 %write_out.1 = (f32[20,8,128]{2,1,0:T(8,128)}, f32[640,1024]{1,0:T(8,128)}) custom-call(f32[20,8,128]{2,1,0:T(8,128)S(1)} %get-tuple-element.6.agg, f32[640,1024]{1,0:T(8,128)S(1)} %get-tuple-element.7.nw), custom_call_target="tpu_custom_call" | custom-call | tf_op jit(solution)/shard_map/write_out/pallas_call | solution.py:542

commit v5 on v4

--- a/solution.py
+++ b/solution.py
@@ -372,12 +372,12 @@
     def arrive(p, slot):
         pltpu.make_async_copy(vs.at[c, p, slot], vs.at[c, p, slot], v_recv.at[p, slot]).wait()
 
-    def forward(p, slot):
+    def forward(p):
         pltpu.make_async_remote_copy(
-            src_ref=vs.at[c, p, slot],
-            dst_ref=vs.at[c, p, slot],
+            src_ref=vs.at[c, p],
+            dst_ref=vs.at[c, p],
             send_sem=f_send,
-            recv_sem=f_recv.at[p, slot],
+            recv_sem=f_recv.at[p],
             device_id=(x, y, 1 - c, z),
             device_id_type=MESH,
         ).start()
@@ -394,7 +394,7 @@
             send(chip, slot, s, 0)
         for s in ring:
             send(chip, slot, 0, s)
-        forward(chip, slot)
+    forward(chip)
 
     wgt_load.wait()
 
@@ -418,7 +418,8 @@
             arrive(p, slot)
             for t in ring:
                 send(p, slot, 0, t)
-            forward(p, slot)
+    for s in ring:
+        forward(source(s, 0))
     for s in (0,) + ring:
         place(c, source(s, 0))
     for s in (0,) + ring:
@@ -426,14 +427,13 @@
             p = source(s, t)
             for slot in range(2):
                 arrive(p, slot)
-                forward(p, slot)
+            forward(p)
             place(c, p)
     for s in (0,) + ring:
         for t in (0,) + ring:
             p = source(t, s)
-            for slot in range(2):
-                other = vs.at[1 - c, p, slot]
-                pltpu.make_async_copy(other, other, f_recv.at[p, slot]).wait()
+            other = vs.at[1 - c, p]
+            pltpu.make_async_copy(other, other, f_recv.at[p]).wait()
             place(1 - c, p)
 
     for cc in range(NC):
@@ -531,7 +531,7 @@
             dma((3,)),
             dma((NX * NY, 2)),
             dma,
-            dma((NX * NY, 2)),
+            dma((NX * NY,)),
             dma,
             dma,
             pltpu.SemaphoreType.REGULAR((4,)),

time: 77.3 us -> 77.2 us (level)
  no operation moved by 1% of the time
where the time goes in v5:
time: 77.2 us; the launch traced here: 77.1 us
  Pallas kernels  75.8 us (98%)
  between operations  1.28 us (2%)
    pallas_call x1, Pallas kernels, per_device(): pl.pallas_call(kernel, out_shape=(jax.ShapeDtypeStruct((OWNED, NZ, COLS),...  74.3 us

profile of v5, /device:TPU:1, one launch (start us, length us, event | category | flops | bytes accessed | tf_op | source)
XLA Modules:
  0.0 77.1 jit_solution(10432899352272643568)
XLA Ops:
  1.3 74.3 %clip.1 = (f32[20,8,128]{2,1,0:T(8,128)S(1)}, f32[640,1024]{1,0:T(8,128)S(1)}) custom-call(bf16[1536,640]{1,0:T(8,128)(2,1)} %hid.1, bf16[1536,128]{1,0:T(8,128)(2,1)} %kg.1, s32[1,1536]{1,0:T(1,128)} %tok.1, s32[1]{0:T(128)S(6)} %copy.11.flag, f32[1,640,1024]{2,1,0:T(8,128)} %mom.1, f32[20,8,128]{2,1,0:T(8,128)} %bitcast.2, f32[640,1024]{1,0:T(8,128)} %wgt.1), custom_call_target="tpu_custom_call" | custom-call | tf_op jit(solution)/shard_map/clip/pallas_call | solution.py:492
  75.6 1.5 %write_out.1 = (f32[20,8,128]{2,1,0:T(8,128)}, f32[640,1024]{1,0:T(8,128)}) custom-call(f32[20,8,128]{2,1,0:T(8,128)S(1)} %get-tuple-element.6.agg, f32[640,1024]{1,0:T(8,128)S(1)} %get-tuple-element.7.nw), custom_call_target="tpu_custom_call" | custom-call | tf_op jit(solution)/shard_map/write_out/pallas_call | solution.py:542
